TPU v7x, 128 devices: a whole 4x4x4 slice. The times are simulated.
128 devices in a mesh: rows: 32 (over x, y, core), grp: 4 (over z).
Axes of the slice: x: 4, y: 4, z: 4, core: 2. Of those that a mesh axis runs over, the one named last changes fastest.
Arguments:
- embeddings: bfloat16 [262144, 1024], P('rows', 'grp'), may hold values from -6 to 6
- fine_local: int32 [262144], P('rows'), may hold values from 0 to 2047
- send_counts: int32 [32, 32], P('rows'), may hold values from 0 to 512, as said below
- old_fine: bfloat16 [65536, 1024], P('rows', 'grp'), may hold values from -6 to 6
- coarse_ids: int32 [65536], P('rows'), may hold values from 0 to 8191, as said below
- old_coarse: bfloat16 [8192, 1024], P('rows', 'grp'), may hold values from -6 to 6
Outputs:
- new_fine: bfloat16 [65536, 1024], P('rows', 'grp')
- coarse_dirs: bfloat16 [8192, 1024], P('rows')
Inputs may be any that keep to these rules, and one draw needn't show every extreme that they name: Row d of send_counts splits the 8192 rows of block d, in order, into segments for owners 0, 1, ...; each row of send_counts sums to 8192; one owner receives exactly 512 rows from every block. `coarse_ids`: within each block of 2048 consecutive level-1 clusters, at most 128 have a level-2 cluster in any one block of 256 consecutive level-2 clusters; one such block reaches that from every block.
All inputs are finite; a program needn't handle non-finite values.
Results may differ from a plain program's by a relative error of at most 0.006.
Values may be sent and summed in bfloat16 or wider, within the bound.
No kernel may reach another device: no remote copies, remote signals or barrier semaphores. Data moves between devices by JAX's collectives and lax.ppermute only.
A program may use at most 64 MiB of HBM per device.

v0:
```python
import math
import jax
import jax.numpy as jnp
from jax import lax
from jax.sharding import PartitionSpec as P


def onehot_sums(arrived, arrived_labels, fine_dev):
    slot_total = arrived.shape[0]
    width = arrived.shape[1]
    block_rows = math.gcd(slot_total, 2048)
    block_count = slot_total // block_rows
    cluster_index = jnp.arange(fine_dev, dtype=jnp.int32)

    def accumulate(state_pair, pieces):
        fine_sums, totals = state_pair
        row_block, label_block = pieces
        onehot = cluster_index[:, None] == label_block[None, :]
        fine_sums = fine_sums + jnp.dot(
            onehot.astype(jnp.bfloat16), row_block, preferred_element_type=jnp.float32
        )
        totals = totals + jnp.sum(onehot.astype(jnp.int32), axis=1)
        return ((fine_sums, totals), None)

    start_state = (jnp.zeros((fine_dev, width), jnp.float32), jnp.zeros((fine_dev,), jnp.int32))
    (fine_sums, totals), _ = lax.scan(
        accumulate,
        start_state,
        (
            arrived.reshape(block_count, block_rows, width),
            arrived_labels.reshape(block_count, block_rows),
        ),
    )
    return (fine_sums, totals.astype(jnp.float32))


def on_device(embeddings, fine_local, send_counts, old_fine, coarse_ids, old_coarse):
    peer_count = lax.axis_size("rows")
    per_dev = embeddings.shape[0]
    quarter = embeddings.shape[1]
    fine_dev = old_fine.shape[0]
    coarse_dev = old_coarse.shape[0]
    capacity = 2 * per_dev // peer_count
    counts = send_counts[0]
    starts = jnp.cumsum(counts) - counts
    offset = jnp.arange(capacity, dtype=jnp.int32)
    is_live = offset[None, :] < counts[:, None]
    padded_rows = jnp.concatenate(
        [embeddings, jnp.zeros((capacity, quarter), jnp.bfloat16)], axis=0
    )
    padded_local = jnp.concatenate([fine_local, jnp.zeros((capacity,), jnp.int32)], axis=0)

    def take_segment(first_row):
        segment_rows = lax.dynamic_slice_in_dim(padded_rows, first_row, capacity, 0)
        segment_labels = lax.dynamic_slice_in_dim(padded_local, first_row, capacity, 0)
        return (segment_rows, segment_labels)

    outgoing, raw_labels = lax.map(take_segment, starts)
    outgoing = jnp.where(is_live[:, :, None], outgoing, jnp.zeros((), jnp.bfloat16))
    labels = jnp.where(is_live, raw_labels, -1)
    arrived, arrived_labels = (
        lax.all_to_all(outgoing, "rows", split_axis=0, concat_axis=0, tiled=True),
        lax.all_to_all(labels, "rows", split_axis=0, concat_axis=0, tiled=True),
    )
    fine_sums, totals = onehot_sums(
        arrived.reshape(-1, quarter), arrived_labels.reshape(-1), fine_dev
    )
    new_fine = ((fine_sums + old_fine.astype(jnp.float32)) / (totals + 1.0)[:, None]).astype(
        jnp.bfloat16
    )
    owners = coarse_ids // coarse_dev
    local_id = coarse_ids - owners * coarse_dev
    capacity_two = 2 * fine_dev // peer_count
    member = (owners[:, None] == jnp.arange(peer_count, dtype=jnp.int32)[None, :]).astype(jnp.int32)
    slot_rank = jnp.sum(jnp.cumsum(member, axis=0) * member, axis=1) - 1
    slot_pos = owners * capacity_two + slot_rank
    placement = (
        jnp.arange(peer_count * capacity_two, dtype=jnp.int32)[:, None] == slot_pos[None, :]
    ).astype(jnp.bfloat16)
    outgoing_two = jnp.dot(placement, new_fine, preferred_element_type=jnp.float32).astype(
        jnp.bfloat16
    )
    label_plus = jnp.dot(
        placement, (local_id + 1).astype(jnp.bfloat16), preferred_element_type=jnp.float32
    )
    labels_two = label_plus.astype(jnp.int32) - 1
    received, received_labels = (
        lax.all_to_all(
            outgoing_two.reshape(peer_count, capacity_two, quarter),
            "rows",
            split_axis=0,
            concat_axis=0,
            tiled=True,
        ),
        lax.all_to_all(
            labels_two.reshape(peer_count, capacity_two),
            "rows",
            split_axis=0,
            concat_axis=0,
            tiled=True,
        ),
    )
    onehot_two = (
        jnp.arange(coarse_dev, dtype=jnp.int32)[:, None] == received_labels.reshape(-1)[None, :]
    )
    coarse_sums = jnp.dot(
        onehot_two.astype(jnp.bfloat16),
        received.reshape(-1, quarter),
        preferred_element_type=jnp.float32,
    )
    coarse_totals = jnp.sum(onehot_two.astype(jnp.int32), axis=1).astype(jnp.float32)
    coarse_means = (coarse_sums + old_coarse.astype(jnp.float32)) / (coarse_totals + 1.0)[:, None]
    full_means = lax.all_gather(coarse_means, "grp", axis=1, tiled=True)
    scale = lax.rsqrt(jnp.mean(full_means * full_means, axis=1, keepdims=True) + 1e-06)
    coarse_dirs = (full_means * scale).astype(jnp.bfloat16)
    return (new_fine, coarse_dirs)


def solution(mesh):
    in_specs = (
        P("rows", "grp"),
        P("rows"),
        P("rows", None),
        P("rows", "grp"),
        P("rows"),
        P("rows", "grp"),
    )
    out_specs = (P("rows", "grp"), P("rows", None))
    return jax.shard_map(
        on_device, mesh=mesh, in_specs=in_specs, out_specs=out_specs, check_vma=False
    )
```

profile of v0, /device:TPU:0, one launch (start us, length us, event | category | flops | bytes accessed | tf_op | source)
XLA Modules:
  0.0 446.7 jit_solution(14028012184819032292)
XLA Ops:
  9.5 3.9 concatenate.6
  13.4 147.6 %while.27 = (s32[]{:T(128)}, bf16[32,512,256]{2,1,0:T(8,128)(2,1)}, s32[32,512]{1,0:T(8,128)S(1)}, s32[32]{0:T(128)S(1)}, bf16[8704,256]{1,0:T(8,128)(2,1)}, /*index=5*/s32[8704]{0:T(1024)S(1)}) while((s32[]{:T(128)}, bf16[32,512,256]{2,1,0:T(8,128)(2,1)}, s32[32,512]{1,0:T(8,128)S(1)}, s32[32]{0:T(128)S(1)}, ...), condition=%wide.region_2.3_spmd.clone, body=%wide.region_1.2_spmd.sunk.clone | while | flops 5 | bytes 533119 | solution.py:58
  16.1 1.7 bitcast_dynamic-update-slice_fusion.3
  20.7 1.7 bitcast_dynamic-update-slice_fusion.3
  25.3 1.7 bitcast_dynamic-update-slice_fusion.3
  29.9 1.7 bitcast_dynamic-update-slice_fusion.3
  34.6 1.7 bitcast_dynamic-update-slice_fusion.3
  39.2 1.7 bitcast_dynamic-update-slice_fusion.3
  43.8 1.7 bitcast_dynamic-update-slice_fusion.3
  48.4 1.7 bitcast_dynamic-update-slice_fusion.3
  53.0 1.7 bitcast_dynamic-update-slice_fusion.3
  57.7 1.7 bitcast_dynamic-update-slice_fusion.3
  62.3 1.7 bitcast_dynamic-update-slice_fusion.3
  66.9 1.7 bitcast_dynamic-update-slice_fusion.3
  71.5 1.7 bitcast_dynamic-update-slice_fusion.3
  76.1 1.7 bitcast_dynamic-update-slice_fusion.3
  80.8 1.7 bitcast_dynamic-update-slice_fusion.3
  85.4 1.7 bitcast_dynamic-update-slice_fusion.3
  90.0 1.7 bitcast_dynamic-update-slice_fusion.3
  94.6 1.7 bitcast_dynamic-update-slice_fusion.3
  99.2 1.7 bitcast_dynamic-update-slice_fusion.3
  103.8 1.7 bitcast_dynamic-update-slice_fusion.3
  108.4 1.7 bitcast_dynamic-update-slice_fusion.3
  113.0 1.7 bitcast_dynamic-update-slice_fusion.3
  117.7 1.7 bitcast_dynamic-update-slice_fusion.3
  122.3 1.7 bitcast_dynamic-update-slice_fusion.3
  126.9 1.7 bitcast_dynamic-update-slice_fusion.3
  131.5 1.7 bitcast_dynamic-update-slice_fusion.3
  136.1 1.7 bitcast_dynamic-update-slice_fusion.3
  140.7 1.7 bitcast_dynamic-update-slice_fusion.3
  145.4 1.7 bitcast_dynamic-update-slice_fusion.3
  150.0 1.7 bitcast_dynamic-update-slice_fusion.3
  154.6 1.7 bitcast_dynamic-update-slice_fusion.3
  159.2 1.7 bitcast_dynamic-update-slice_fusion.3
  161.8 7.4 %all-to-all-start = ((s32[32,1,512]{2,1,0:T(1,128)}), s32[32,1,512]{2,1,0:T(1,128)S(1)}, u32[]{:S(2)}, u32[]{:S(2)}) async-start(s32[32,1,512]{2,1,0:T(1,128)} %all_to_all.18), calls=%async_computation | async-start | bytes 131072 | tf_op jit(solution)/shard_map/all_to_all | solution.py:63
  169.3 8.1 %broadcast_select_fusion = bf16[32,512,256]{2,1,0:T(8,128)(2,1)} fusion(bf16[32,512,256]{2,1,0:T(8,128)(2,1)} %get-tuple-element.69, pred[32,512]{1,0:T(8,128)(4,1)S(1)} %iota_compare_fusion.17), kind=kLoop, calls=%fused_computation.18 | loop fusion | flops 4194304 | bytes 16793600 | tf_op jit(solution)/shard_map/jit(_where)/select_n | solution.py:59
  177.4 7.6 %all-to-all-start.1 = ((bf16[32,512,256]{2,1,0:T(8,128)(2,1)}), bf16[32,512,256]{2,1,0:T(8,128)(2,1)}, u32[]{:S(2)}, u32[]{:S(2)}) async-start(bf16[32,512,256]{2,1,0:T(8,128)(2,1)} %broadcast_select_fusion), calls=%async_computation.1 | async-start | bytes 16777216 | tf_op jit(solution)/shard_map/all_to_all | solution.py:62
  185.1 9.1 %reduce-window.20 = s32[32,16,128]{2,1,0:T(8,128)S(1)} reduce-window(s32[32,16,128]{2,1,0:T(8,128)S(1)} %fusion.21, s32[]{:T(128)} %copy.41), window={size=1x1x128 pad=0_0x0_0x127_0}, to_apply=%region_6.7 | reduce-window | flops 8323072 | bytes 524292 | tf_op jit(solution)/shard_map/reduce-window.1
  195.1 5.6 %fusion.11 = f32[1,4096]{1,0:T(1,128)S(1)} fusion(bf16[2048,1]{0,1:T(2,128)(2,1)S(1)} %reshape.106, s32[2048]{0:T(1024)S(1)} %get-tuple-element.115), kind=kOutput, calls=%fused_computation.15 | convolution fusion | flops 25165824 | bytes 28672 | tf_op jit(solution)/shard_map/dot_general | solution.py:83
  201.5 97.1 %all-to-all-done.1 = bf16[32,512,256]{2,1,0:T(8,128)(2,1)} async-done(((bf16[32,512,256]{2,1,0:T(8,128)(2,1)}), bf16[32,512,256]{2,1,0:T(8,128)(2,1)}, u32[]{:S(2)}, u32[]{:S(2)}) %all-to-all-start.1) | async-done | bytes 8388640 | tf_op jit(solution)/shard_map/all_to_all | solution.py:62
  298.6 14.2 %all-to-all-start.2 = ((s32[32,1,128]{2,1,0:T(1,128)}), s32[32,1,128]{2,1,0:T(1,128)S(1)}, u32[]{:S(2)}, u32[]{:S(2)}) async-start(s32[32,1,128]{2,1,0:T(1,128)} %bitcast.11), calls=%async_computation.2 | async-start | bytes 32768 | tf_op jit(solution)/shard_map/all_to_all | solution.py:95
  312.8 54.2 %while.28 = (s32[]{:T(128)}, f32[2048,256]{1,0:T(8,128)S(1)}, s32[2048]{0:T(1024)S(1)}, s32[8,2048]{1,0:T(8,128)S(1)}, bf16[8,2048,256]{2,1,0:T(8,128)(2,1)}) while((s32[]{:T(128)}, f32[2048,256]{1,0:T(8,128)S(1)}, s32[2048]{0:T(1024)S(1)}, s32[8,2048]{1,0:T(8,128)S(1)}, bf16[8,2048,256]{2,1,0:T(8,128)(2,1)}) %tuple.50), condition=%wide.region_5.6_spmd.clone.clone, body=%wide.region_3.5_spmd.clone.sunk.clone | while | flops 2165311488 | bytes 5309004 | solution.py:26
  312.8 5.1 %fusion.35 = f32[2048,256]{1,0:T(8,128)S(1)} fusion(s32[2048]{0:T(1024)S(1)} %bitcast.55, f32[2048,256]{1,0:T(8,128)S(1)} %get-tuple-element.239, bf16[8,2048,256]{2,1,0:T(8,128)(2,1)} %get-tuple-element.247, s32[]{:T(128)} %get-tuple-element.238, pred[]{:T(512)S(6)} %compare.8), kind=kOutput, calls=%fused_computation.7.clone.1.clone | convolution fusion | flops 2152726528 | bytes 5251585 | tf_op jit(solution)/shard_map/while/body/eval_jaxpr/dot_general | solution.py:19
  317.9 1.7 fusion.36
  319.7 5.0 %fusion.35 = f32[2048,256]{1,0:T(8,128)S(1)} fusion(s32[2048]{0:T(1024)S(1)} %bitcast.55, f32[2048,256]{1,0:T(8,128)S(1)} %get-tuple-element.239, bf16[8,2048,256]{2,1,0:T(8,128)(2,1)} %get-tuple-element.247, s32[]{:T(128)} %get-tuple-element.238, pred[]{:T(512)S(6)} %compare.8), kind=kOutput, calls=%fused_computation.7.clone.1.clone | convolution fusion | flops 2152726528 | bytes 5251585 | tf_op jit(solution)/shard_map/while/body/eval_jaxpr/dot_general | solution.py:19
  324.7 1.7 fusion.36
  326.4 5.0 %fusion.35 = f32[2048,256]{1,0:T(8,128)S(1)} fusion(s32[2048]{0:T(1024)S(1)} %bitcast.55, f32[2048,256]{1,0:T(8,128)S(1)} %get-tuple-element.239, bf16[8,2048,256]{2,1,0:T(8,128)(2,1)} %get-tuple-element.247, s32[]{:T(128)} %get-tuple-element.238, pred[]{:T(512)S(6)} %compare.8), kind=kOutput, calls=%fused_computation.7.clone.1.clone | convolution fusion | flops 2152726528 | bytes 5251585 | tf_op jit(solution)/shard_map/while/body/eval_jaxpr/dot_general | solution.py:19
  331.4 1.7 fusion.36
  333.2 5.0 %fusion.35 = f32[2048,256]{1,0:T(8,128)S(1)} fusion(s32[2048]{0:T(1024)S(1)} %bitcast.55, f32[2048,256]{1,0:T(8,128)S(1)} %get-tuple-element.239, bf16[8,2048,256]{2,1,0:T(8,128)(2,1)} %get-tuple-element.247, s32[]{:T(128)} %get-tuple-element.238, pred[]{:T(512)S(6)} %compare.8), kind=kOutput, calls=%fused_computation.7.clone.1.clone | convolution fusion | flops 2152726528 | bytes 5251585 | tf_op jit(solution)/shard_map/while/body/eval_jaxpr/dot_general | solution.py:19
  338.2 1.7 fusion.36
  340.0 5.0 %fusion.35 = f32[2048,256]{1,0:T(8,128)S(1)} fusion(s32[2048]{0:T(1024)S(1)} %bitcast.55, f32[2048,256]{1,0:T(8,128)S(1)} %get-tuple-element.239, bf16[8,2048,256]{2,1,0:T(8,128)(2,1)} %get-tuple-element.247, s32[]{:T(128)} %get-tuple-element.238, pred[]{:T(512)S(6)} %compare.8), kind=kOutput, calls=%fused_computation.7.clone.1.clone | convolution fusion | flops 2152726528 | bytes 5251585 | tf_op jit(solution)/shard_map/while/body/eval_jaxpr/dot_general | solution.py:19
  345.0 1.7 fusion.36
  346.7 5.0 %fusion.35 = f32[2048,256]{1,0:T(8,128)S(1)} fusion(s32[2048]{0:T(1024)S(1)} %bitcast.55, f32[2048,256]{1,0:T(8,128)S(1)} %get-tuple-element.239, bf16[8,2048,256]{2,1,0:T(8,128)(2,1)} %get-tuple-element.247, s32[]{:T(128)} %get-tuple-element.238, pred[]{:T(512)S(6)} %compare.8), kind=kOutput, calls=%fused_computation.7.clone.1.clone | convolution fusion | flops 2152726528 | bytes 5251585 | tf_op jit(solution)/shard_map/while/body/eval_jaxpr/dot_general | solution.py:19
  351.7 1.7 fusion.36
  353.5 5.0 %fusion.35 = f32[2048,256]{1,0:T(8,128)S(1)} fusion(s32[2048]{0:T(1024)S(1)} %bitcast.55, f32[2048,256]{1,0:T(8,128)S(1)} %get-tuple-element.239, bf16[8,2048,256]{2,1,0:T(8,128)(2,1)} %get-tuple-element.247, s32[]{:T(128)} %get-tuple-element.238, pred[]{:T(512)S(6)} %compare.8), kind=kOutput, calls=%fused_computation.7.clone.1.clone | convolution fusion | flops 2152726528 | bytes 5251585 | tf_op jit(solution)/shard_map/while/body/eval_jaxpr/dot_general | solution.py:19
  358.5 1.7 fusion.36
  360.3 5.0 %fusion.35 = f32[2048,256]{1,0:T(8,128)S(1)} fusion(s32[2048]{0:T(1024)S(1)} %bitcast.55, f32[2048,256]{1,0:T(8,128)S(1)} %get-tuple-element.239, bf16[8,2048,256]{2,1,0:T(8,128)(2,1)} %get-tuple-element.247, s32[]{:T(128)} %get-tuple-element.238, pred[]{:T(512)S(6)} %compare.8), kind=kOutput, calls=%fused_computation.7.clone.1.clone | convolution fusion | flops 2152726528 | bytes 5251585 | tf_op jit(solution)/shard_map/while/body/eval_jaxpr/dot_general | solution.py:19
  365.2 1.7 fusion.36
  368.4 7.4 %fusion.14 = bf16[4096,256]{1,0:T(8,128)(2,1)} fusion(bf16[2048,256]{1,0:T(8,128)(2,1)S(1)} %divide_convert_fusion, s32[2048]{0:T(1024)S(1)} %get-tuple-element.115), kind=kOutput, calls=%fused_computation.19 | convolution fusion | flops 4304404480 | bytes 3153920 | tf_op jit(solution)/shard_map/dot_general | solution.py:80
  375.8 7.3 %all-to-all-start.3 = ((bf16[32,128,256]{2,1,0:T(8,128)(2,1)}), bf16[32,128,256]{2,1,0:T(8,128)(2,1)S(1)}, u32[]{:S(2)}, u32[]{:S(2)}) async-start(bf16[32,128,256]{2,1,0:T(8,128)(2,1)} %bitcast.13), calls=%async_computation.3 | async-start | bytes 4194304 | tf_op jit(solution)/shard_map/all_to_all | solution.py:88
  383.7 28.4 %all-to-all-done.3 = bf16[32,128,256]{2,1,0:T(8,128)(2,1)S(1)} async-done(((bf16[32,128,256]{2,1,0:T(8,128)(2,1)}), bf16[32,128,256]{2,1,0:T(8,128)(2,1)S(1)}, u32[]{:S(2)}, u32[]{:S(2)}) %all-to-all-start.3) | async-done | bytes 2097184 | tf_op jit(solution)/shard_map/all_to_all | solution.py:88
  412.1 1.4 fusion.18
  413.6 22.8 %all-gather.2.cloned.1.call-done = f32[256,1024]{1,0:T(8,128)} async-done(((f32[256,256]{1,0:T(8,128)}), f32[256,1024]{1,0:T(8,128)}) %all-gather.2.cloned.1.call-update) | async-done | bytes 1048592 | tf_op jit(solution)/shard_map/all_gather | solution.py:113
  437.7 2.1 multiply_convert_fusion
  (156 shorter events, 33.2 us)
Async XLA Ops:
  9.5 151.5 %copy-start.3 = (s32[1,32]{1,0:T(1,128)S(1)}, s32[1,32]{1,0:T(1,128)}, u32[]{:S(2)}) copy-start(s32[1,32]{1,0:T(1,128)} %param.12) | copy-start | bytes 388
  161.8 15.6 %all-to-all-start = ((s32[32,1,512]{2,1,0:T(1,128)}), s32[32,1,512]{2,1,0:T(1,128)S(1)}, u32[]{:S(2)}, u32[]{:S(2)}) async-start(s32[32,1,512]{2,1,0:T(1,128)} %all_to_all.18), calls=%async_computation | async-start | bytes 131072 | tf_op jit(solution)/shard_map/all_to_all | solution.py:63
  177.4 7.7 %copy-start.2 = (s32[2048]{0:T(1024)S(1)}, s32[2048]{0:T(1024)}, u32[]{:S(2)}) copy-start(s32[2048]{0:T(1024)} %param.14) | copy-start | bytes 24580
  177.4 121.2 %all-to-all-start.1 = ((bf16[32,512,256]{2,1,0:T(8,128)(2,1)}), bf16[32,512,256]{2,1,0:T(8,128)(2,1)}, u32[]{:S(2)}, u32[]{:S(2)}) async-start(bf16[32,512,256]{2,1,0:T(8,128)(2,1)} %broadcast_select_fusion), calls=%async_computation.1 | async-start | bytes 16777216 | tf_op jit(solution)/shard_map/all_to_all | solution.py:62
  298.6 77.3 %all-to-all-start.2 = ((s32[32,1,128]{2,1,0:T(1,128)}), s32[32,1,128]{2,1,0:T(1,128)S(1)}, u32[]{:S(2)}, u32[]{:S(2)}) async-start(s32[32,1,128]{2,1,0:T(1,128)} %bitcast.11), calls=%async_computation.2 | async-start | bytes 32768 | tf_op jit(solution)/shard_map/all_to_all | solution.py:95
  312.8 54.2 %copy-start = (bf16[2048,256]{1,0:T(8,128)(2,1)S(1)}, bf16[2048,256]{1,0:T(8,128)(2,1)}, u32[]{:S(2)}) copy-start(bf16[2048,256]{1,0:T(8,128)(2,1)} %param.13) | copy-start | bytes 3145732
  367.4 1.0 copy-start.1
  375.8 36.3 %copy-start.4 = (bf16[256,256]{1,0:T(8,128)(2,1)S(1)}, bf16[256,256]{1,0:T(8,128)(2,1)}, u32[]{:S(2)}) copy-start(bf16[256,256]{1,0:T(8,128)(2,1)} %param.15) | copy-start | bytes 393220
  375.8 36.3 %all-to-all-start.3 = ((bf16[32,128,256]{2,1,0:T(8,128)(2,1)}), bf16[32,128,256]{2,1,0:T(8,128)(2,1)S(1)}, u32[]{:S(2)}, u32[]{:S(2)}) async-start(bf16[32,128,256]{2,1,0:T(8,128)(2,1)} %bitcast.13), calls=%async_computation.3 | async-start | bytes 4194304 | tf_op jit(solution)/shard_map/all_to_all | solution.py:88
  383.2 53.1 %all-gather.2.cloned.1.call-start = ((), (), s32[]{:S(2)}) async-start(), calls=%async_computation.4 | async-start | bytes 1310720 | tf_op jit(solution)/shard_map/all_gather | solution.py:113
Sparse Core Ops, SparseCore 0:
  413.7 22.5 all-gather.1
where the time goes:
time: 450 us; the launch traced here: 447 us
  waiting for transfers between devices  148 us (33%)
  local copies, waits for them, and re-layouts  87.8 us (20%)
  loops' own time  67.7 us (15%)
  matrix products  54.3 us (12%)
  other arithmetic  37.7 us (8%)
  starting transfers between devices  36.7 us (8%)
  between operations  14.2 us (3%)
    all_to_all x1, waiting for transfers between devices, on_device(): lax.all_to_all(outgoing, 'rows', split_axis=0, concat_axis=0, tiled=True)  97.1 us
    another operation x1, loops' own time, on_device(): outgoing, raw_labels = lax.map(take_segment, starts)  67.3 us
    dynamic_update_slice x64, local copies, waits for them, and re-layouts, on_device(): outgoing, raw_labels = lax.map(take_segment, starts)  56.5 us
    dot_general x8, matrix products, accumulate(): jnp.dot(onehot.astype(jnp.bfloat16), row_block, preferred_element_type=jn...  39.8 us
    all_to_all x1, waiting for transfers between devices, on_device(): lax.all_to_all(outgoing_two.reshape(peer_count, capacity_two, quarter), '...  28.4 us
    all_gather x1, waiting for transfers between devices, on_device(): full_means = lax.all_gather(coarse_means, 'grp', axis=1, tiled=True)  22.8 us
    dynamic_slice x32, local copies, waits for them, and re-layouts, on_device(): outgoing, raw_labels = lax.map(take_segment, starts)  21.4 us
    all_to_all x1, starting transfers between devices, on_device(): lax.all_to_all(labels_two.reshape(peer_count, capacity_two), 'rows', spli...  14.2 us
  transfers between devices with their start and end apart: 5, of which 3 were waited for; matrix products, arithmetic and copies ran while one was open for 19% of the time, Pallas kernels for 0%

commit v1 on v0

--- a/solution.py
+++ b/solution.py
@@ -1,8 +1,22 @@
+import functools
 import math
 import jax
 import jax.numpy as jnp
 from jax import lax
 from jax.sharding import PartitionSpec as P
+
+
+def lift_knots(packet, mesh_ax):
+    found = []
+    for _ in range(lax.axis_size(mesh_ax)):
+        found.append(packet)
+    d_next = jnp.stack(found)
+    p_next = lax.all_to_all(d_next, concat_axis=0, axis_name=mesh_ax, split_axis=0)
+    reached = jnp.concatenate(p_next, 1)
+    return reached
+
+
+apply_kinds_on_mesh = functools.partial(lift_knots, mesh_ax="grp")
 
 
 def onehot_sums(arrived, arrived_labels, fine_dev):
@@ -110,7 +124,7 @@
     )
     coarse_totals = jnp.sum(onehot_two.astype(jnp.int32), axis=1).astype(jnp.float32)
     coarse_means = (coarse_sums + old_coarse.astype(jnp.float32)) / (coarse_totals + 1.0)[:, None]
-    full_means = lax.all_gather(coarse_means, "grp", axis=1, tiled=True)
+    full_means = apply_kinds_on_mesh(coarse_means)
     scale = lax.rsqrt(jnp.mean(full_means * full_means, axis=1, keepdims=True) + 1e-06)
     coarse_dirs = (full_means * scale).astype(jnp.bfloat16)
     return (new_fine, coarse_dirs)

time: 450 us -> 431 us (0.958)
  waiting for transfers between devices: 148 us -> 126 us
  blocking collectives: 0 us -> 20.1 us
  between operations: 14.2 us -> 0.87 us
    all_gather x1 -> x0, waiting for transfers between devices: 22.8 us -> none  [on_device(): full_means = lax.all_gather(coarse_means, 'grp', axis=1, tiled=True)]
    all_to_all x0 -> x1, blocking collectives: none -> 20.1 us  [lift_knots(): lax.all_to_all(d_next, concat_axis=0, axis_name=mesh_ax, split_axis=0)]
  transfers between devices with their start and end apart: 5 -> 4, of which waited for: 3 -> 2; matrix products, arithmetic and copies ran while one was open for 19% -> 20% of each run, Pallas kernels for 0% -> 0%
where the time goes in v1:
time: 431 us; the launch traced here: 428 us
  waiting for transfers between devices  126 us (29%)
  local copies, waits for them, and re-layouts  89.2 us (21%)
  loops' own time  67.7 us (16%)
  matrix products  53.6 us (12%)
  starting transfers between devices  36.7 us (9%)
  other arithmetic  34.5 us (8%)
  blocking collectives  20.1 us (5%)
    all_to_all x1, waiting for transfers between devices, on_device(): lax.all_to_all(outgoing, 'rows', split_axis=0, concat_axis=0, tiled=True)  97.1 us
    another operation x1, loops' own time, on_device(): outgoing, raw_labels = lax.map(take_segment, starts)  67.3 us
    dynamic_update_slice x64, local copies, waits for them, and re-layouts, on_device(): outgoing, raw_labels = lax.map(take_segment, starts)  56.5 us
    dot_general x8, matrix products, accumulate(): jnp.dot(onehot.astype(jnp.bfloat16), row_block, preferred_element_type=jn...  39.8 us
    all_to_all x1, waiting for transfers between devices, on_device(): lax.all_to_all(outgoing_two.reshape(peer_count, capacity_two, quarter), '...  28.4 us
    dynamic_slice x32, local copies, waits for them, and re-layouts, on_device(): outgoing, raw_labels = lax.map(take_segment, starts)  21.4 us
    all_to_all x1, blocking collectives, lift_knots(): lax.all_to_all(d_next, concat_axis=0, axis_name=mesh_ax, split_axis=0)  20.1 us
    all_to_all x1, starting transfers between devices, on_device(): lax.all_to_all(labels_two.reshape(peer_count, capacity_two), 'rows', spli...  14.2 us
  transfers between devices with their start and end apart: 4, of which 2 were waited for; matrix products, arithmetic and copies ran while one was open for 20% of the time, Pallas kernels for 0%

profile of v1, /device:TPU:0, one launch (start us, length us, event | category | flops | bytes accessed | tf_op | source)
XLA Modules:
  0.0 428.1 jit_solution(3371059451216407386)
XLA Ops:
  3.0 3.9 concatenate.6
  6.9 147.6 %while.27 = (s32[]{:T(128)}, bf16[32,512,256]{2,1,0:T(8,128)(2,1)}, s32[32,512]{1,0:T(8,128)S(1)}, s32[32]{0:T(128)S(1)}, bf16[8704,256]{1,0:T(8,128)(2,1)}, /*index=5*/s32[8704]{0:T(1024)S(1)}) while((s32[]{:T(128)}, bf16[32,512,256]{2,1,0:T(8,128)(2,1)}, s32[32,512]{1,0:T(8,128)S(1)}, s32[32]{0:T(128)S(1)}, ...), condition=%wide.region_2.3_spmd.clone, body=%wide.region_1.2_spmd.sunk.clone | while | flops 5 | bytes 533119 | solution.py:72
  9.6 1.7 bitcast_dynamic-update-slice_fusion.3
  14.2 1.7 bitcast_dynamic-update-slice_fusion.3
  18.8 1.7 bitcast_dynamic-update-slice_fusion.3
  23.4 1.7 bitcast_dynamic-update-slice_fusion.3
  28.0 1.7 bitcast_dynamic-update-slice_fusion.3
  32.7 1.7 bitcast_dynamic-update-slice_fusion.3
  37.3 1.7 bitcast_dynamic-update-slice_fusion.3
  41.9 1.7 bitcast_dynamic-update-slice_fusion.3
  46.5 1.7 bitcast_dynamic-update-slice_fusion.3
  51.1 1.7 bitcast_dynamic-update-slice_fusion.3
  55.7 1.7 bitcast_dynamic-update-slice_fusion.3
  60.4 1.7 bitcast_dynamic-update-slice_fusion.3
  65.0 1.7 bitcast_dynamic-update-slice_fusion.3
  69.6 1.7 bitcast_dynamic-update-slice_fusion.3
  74.2 1.7 bitcast_dynamic-update-slice_fusion.3
  78.8 1.7 bitcast_dynamic-update-slice_fusion.3
  83.4 1.7 bitcast_dynamic-update-slice_fusion.3
  88.0 1.7 bitcast_dynamic-update-slice_fusion.3
  92.6 1.7 bitcast_dynamic-update-slice_fusion.3
  97.3 1.7 bitcast_dynamic-update-slice_fusion.3
  101.9 1.7 bitcast_dynamic-update-slice_fusion.3
  106.5 1.7 bitcast_dynamic-update-slice_fusion.3
  111.1 1.7 bitcast_dynamic-update-slice_fusion.3
  115.7 1.7 bitcast_dynamic-update-slice_fusion.3
  120.4 1.7 bitcast_dynamic-update-slice_fusion.3
  125.0 1.7 bitcast_dynamic-update-slice_fusion.3
  129.6 1.7 bitcast_dynamic-update-slice_fusion.3
  134.2 1.7 bitcast_dynamic-update-slice_fusion.3
  138.8 1.7 bitcast_dynamic-update-slice_fusion.3
  143.4 1.7 bitcast_dynamic-update-slice_fusion.3
  148.0 1.7 bitcast_dynamic-update-slice_fusion.3
  152.6 1.7 bitcast_dynamic-update-slice_fusion.3
  155.3 7.4 %all-to-all-start = ((s32[32,1,512]{2,1,0:T(1,128)}), s32[32,1,512]{2,1,0:T(1,128)S(1)}, u32[]{:S(2)}, u32[]{:S(2)}) async-start(s32[32,1,512]{2,1,0:T(1,128)} %all_to_all.21), calls=%async_computation | async-start | bytes 131072 | tf_op jit(solution)/shard_map/all_to_all | solution.py:77
  162.8 8.1 %broadcast_select_fusion = bf16[32,512,256]{2,1,0:T(8,128)(2,1)} fusion(bf16[32,512,256]{2,1,0:T(8,128)(2,1)} %get-tuple-element.69, pred[32,512]{1,0:T(8,128)(4,1)S(1)} %iota_compare_fusion.17), kind=kLoop, calls=%fused_computation.18 | loop fusion | flops 4194304 | bytes 16793600 | tf_op jit(solution)/shard_map/jit(_where)/select_n | solution.py:73
  170.9 7.7 %all-to-all-start.1 = ((bf16[32,512,256]{2,1,0:T(8,128)(2,1)}), bf16[32,512,256]{2,1,0:T(8,128)(2,1)}, u32[]{:S(2)}, u32[]{:S(2)}) async-start(bf16[32,512,256]{2,1,0:T(8,128)(2,1)} %broadcast_select_fusion), calls=%async_computation.1 | async-start | bytes 16777216 | tf_op jit(solution)/shard_map/all_to_all | solution.py:76
  178.6 9.1 %reduce-window.20 = s32[32,16,128]{2,1,0:T(8,128)S(1)} reduce-window(s32[32,16,128]{2,1,0:T(8,128)S(1)} %fusion.23, s32[]{:T(128)} %copy.48), window={size=1x1x128 pad=0_0x0_0x127_0}, to_apply=%region_6.7 | reduce-window | flops 8323072 | bytes 524292 | tf_op jit(solution)/shard_map/reduce-window.1
  188.5 5.6 %fusion.11 = f32[1,4096]{1,0:T(1,128)S(1)} fusion(bf16[2048,1]{0,1:T(2,128)(2,1)S(1)} %reshape.116, s32[2048]{0:T(1024)S(1)} %get-tuple-element.119), kind=kOutput, calls=%fused_computation.15 | convolution fusion | flops 25165824 | bytes 28672 | tf_op jit(solution)/shard_map/dot_general | solution.py:97
  194.9 97.1 %all-to-all-done.1 = bf16[32,512,256]{2,1,0:T(8,128)(2,1)} async-done(((bf16[32,512,256]{2,1,0:T(8,128)(2,1)}), bf16[32,512,256]{2,1,0:T(8,128)(2,1)}, u32[]{:S(2)}, u32[]{:S(2)}) %all-to-all-start.1) | async-done | bytes 8388640 | tf_op jit(solution)/shard_map/all_to_all | solution.py:76
  292.0 14.2 %all-to-all-start.2 = ((s32[32,1,128]{2,1,0:T(1,128)}), s32[32,1,128]{2,1,0:T(1,128)S(1)}, u32[]{:S(2)}, u32[]{:S(2)}) async-start(s32[32,1,128]{2,1,0:T(1,128)} %bitcast.11), calls=%async_computation.2 | async-start | bytes 32768 | tf_op jit(solution)/shard_map/all_to_all | solution.py:109
  306.3 54.2 %while.28 = (s32[]{:T(128)}, f32[2048,256]{1,0:T(8,128)S(1)}, s32[2048]{0:T(1024)S(1)}, s32[8,2048]{1,0:T(8,128)S(1)}, bf16[8,2048,256]{2,1,0:T(8,128)(2,1)}) while((s32[]{:T(128)}, f32[2048,256]{1,0:T(8,128)S(1)}, s32[2048]{0:T(1024)S(1)}, s32[8,2048]{1,0:T(8,128)S(1)}, bf16[8,2048,256]{2,1,0:T(8,128)(2,1)}) %tuple.52), condition=%wide.region_5.6_spmd.clone.clone, body=%wide.region_3.5_spmd.clone.sunk.clone | while | flops 2165311488 | bytes 5309004 | solution.py:40
  306.3 5.1 %fusion.37 = f32[2048,256]{1,0:T(8,128)S(1)} fusion(s32[2048]{0:T(1024)S(1)} %bitcast.64, f32[2048,256]{1,0:T(8,128)S(1)} %get-tuple-element.243, bf16[8,2048,256]{2,1,0:T(8,128)(2,1)} %get-tuple-element.251, s32[]{:T(128)} %get-tuple-element.242, pred[]{:T(512)S(6)} %compare.8), kind=kOutput, calls=%fused_computation.7.clone.1.clone | convolution fusion | flops 2152726528 | bytes 5251585 | tf_op jit(solution)/shard_map/while/body/eval_jaxpr/dot_general | solution.py:33
  311.4 1.7 fusion.38
  313.2 5.0 %fusion.37 = f32[2048,256]{1,0:T(8,128)S(1)} fusion(s32[2048]{0:T(1024)S(1)} %bitcast.64, f32[2048,256]{1,0:T(8,128)S(1)} %get-tuple-element.243, bf16[8,2048,256]{2,1,0:T(8,128)(2,1)} %get-tuple-element.251, s32[]{:T(128)} %get-tuple-element.242, pred[]{:T(512)S(6)} %compare.8), kind=kOutput, calls=%fused_computation.7.clone.1.clone | convolution fusion | flops 2152726528 | bytes 5251585 | tf_op jit(solution)/shard_map/while/body/eval_jaxpr/dot_general | solution.py:33
  318.1 1.7 fusion.38
  319.9 5.0 %fusion.37 = f32[2048,256]{1,0:T(8,128)S(1)} fusion(s32[2048]{0:T(1024)S(1)} %bitcast.64, f32[2048,256]{1,0:T(8,128)S(1)} %get-tuple-element.243, bf16[8,2048,256]{2,1,0:T(8,128)(2,1)} %get-tuple-element.251, s32[]{:T(128)} %get-tuple-element.242, pred[]{:T(512)S(6)} %compare.8), kind=kOutput, calls=%fused_computation.7.clone.1.clone | convolution fusion | flops 2152726528 | bytes 5251585 | tf_op jit(solution)/shard_map/while/body/eval_jaxpr/dot_general | solution.py:33
  324.9 1.7 fusion.38
  326.7 5.0 %fusion.37 = f32[2048,256]{1,0:T(8,128)S(1)} fusion(s32[2048]{0:T(1024)S(1)} %bitcast.64, f32[2048,256]{1,0:T(8,128)S(1)} %get-tuple-element.243, bf16[8,2048,256]{2,1,0:T(8,128)(2,1)} %get-tuple-element.251, s32[]{:T(128)} %get-tuple-element.242, pred[]{:T(512)S(6)} %compare.8), kind=kOutput, calls=%fused_computation.7.clone.1.clone | convolution fusion | flops 2152726528 | bytes 5251585 | tf_op jit(solution)/shard_map/while/body/eval_jaxpr/dot_general | solution.py:33
  331.7 1.7 fusion.38
  333.4 5.0 %fusion.37 = f32[2048,256]{1,0:T(8,128)S(1)} fusion(s32[2048]{0:T(1024)S(1)} %bitcast.64, f32[2048,256]{1,0:T(8,128)S(1)} %get-tuple-element.243, bf16[8,2048,256]{2,1,0:T(8,128)(2,1)} %get-tuple-element.251, s32[]{:T(128)} %get-tuple-element.242, pred[]{:T(512)S(6)} %compare.8), kind=kOutput, calls=%fused_computation.7.clone.1.clone | convolution fusion | flops 2152726528 | bytes 5251585 | tf_op jit(solution)/shard_map/while/body/eval_jaxpr/dot_general | solution.py:33
  338.4 1.7 fusion.38
  340.2 5.0 %fusion.37 = f32[2048,256]{1,0:T(8,128)S(1)} fusion(s32[2048]{0:T(1024)S(1)} %bitcast.64, f32[2048,256]{1,0:T(8,128)S(1)} %get-tuple-element.243, bf16[8,2048,256]{2,1,0:T(8,128)(2,1)} %get-tuple-element.251, s32[]{:T(128)} %get-tuple-element.242, pred[]{:T(512)S(6)} %compare.8), kind=kOutput, calls=%fused_computation.7.clone.1.clone | convolution fusion | flops 2152726528 | bytes 5251585 | tf_op jit(solution)/shard_map/while/body/eval_jaxpr/dot_general | solution.py:33
  345.2 1.7 fusion.38
  347.0 5.0 %fusion.37 = f32[2048,256]{1,0:T(8,128)S(1)} fusion(s32[2048]{0:T(1024)S(1)} %bitcast.64, f32[2048,256]{1,0:T(8,128)S(1)} %get-tuple-element.243, bf16[8,2048,256]{2,1,0:T(8,128)(2,1)} %get-tuple-element.251, s32[]{:T(128)} %get-tuple-element.242, pred[]{:T(512)S(6)} %compare.8), kind=kOutput, calls=%fused_computation.7.clone.1.clone | convolution fusion | flops 2152726528 | bytes 5251585 | tf_op jit(solution)/shard_map/while/body/eval_jaxpr/dot_general | solution.py:33
  352.0 1.7 fusion.38
  353.7 5.0 %fusion.37 = f32[2048,256]{1,0:T(8,128)S(1)} fusion(s32[2048]{0:T(1024)S(1)} %bitcast.64, f32[2048,256]{1,0:T(8,128)S(1)} %get-tuple-element.243, bf16[8,2048,256]{2,1,0:T(8,128)(2,1)} %get-tuple-element.251, s32[]{:T(128)} %get-tuple-element.242, pred[]{:T(512)S(6)} %compare.8), kind=kOutput, calls=%fused_computation.7.clone.1.clone | convolution fusion | flops 2152726528 | bytes 5251585 | tf_op jit(solution)/shard_map/while/body/eval_jaxpr/dot_general | solution.py:33
  358.7 1.7 fusion.38
  360.9 1.0 copy-done.1
  361.9 7.4 %fusion.14 = bf16[4096,256]{1,0:T(8,128)(2,1)} fusion(bf16[2048,256]{1,0:T(8,128)(2,1)S(1)} %divide_convert_fusion, s32[2048]{0:T(1024)S(1)} %get-tuple-element.119), kind=kOutput, calls=%fused_computation.19 | convolution fusion | flops 4304404480 | bytes 3153920 | tf_op jit(solution)/shard_map/dot_general | solution.py:94
  369.3 7.3 %all-to-all-start.3 = ((bf16[32,128,256]{2,1,0:T(8,128)(2,1)}), bf16[32,128,256]{2,1,0:T(8,128)(2,1)S(1)}, u32[]{:S(2)}, u32[]{:S(2)}) async-start(bf16[32,128,256]{2,1,0:T(8,128)(2,1)} %bitcast.13), calls=%async_computation.3 | async-start | bytes 4194304 | tf_op jit(solution)/shard_map/all_to_all | solution.py:102
  377.2 28.4 %all-to-all-done.3 = bf16[32,128,256]{2,1,0:T(8,128)(2,1)S(1)} async-done(((bf16[32,128,256]{2,1,0:T(8,128)(2,1)}), bf16[32,128,256]{2,1,0:T(8,128)(2,1)S(1)}, u32[]{:S(2)}, u32[]{:S(2)}) %all-to-all-start.3) | async-done | bytes 2097184 | tf_op jit(solution)/shard_map/all_to_all | solution.py:102
  406.4 20.1 %all_to_all.33 = f32[4,256,256]{2,1,0:T(8,128)S(1)} all-to-all(f32[4,256,256]{2,1,0:T(8,128)S(1)} %stack.2), channel_id=1, replica_groups=mesh['rows'=32,'grp'=4] {'grp'}, dimensions={0} | all-to-all | bytes 2097152 | tf_op jit(solution)/shard_map/all_to_all | solution.py:14
  427.0 1.0 copy.24
  (157 shorter events, 32.2 us)
Async XLA Ops:
  3.0 151.5 %copy-start.3 = (s32[1,32]{1,0:T(1,128)S(1)}, s32[1,32]{1,0:T(1,128)}, u32[]{:S(2)}) copy-start(s32[1,32]{1,0:T(1,128)} %param.12) | copy-start | bytes 388
  155.3 15.6 %all-to-all-start = ((s32[32,1,512]{2,1,0:T(1,128)}), s32[32,1,512]{2,1,0:T(1,128)S(1)}, u32[]{:S(2)}, u32[]{:S(2)}) async-start(s32[32,1,512]{2,1,0:T(1,128)} %all_to_all.21), calls=%async_computation | async-start | bytes 131072 | tf_op jit(solution)/shard_map/all_to_all | solution.py:77
  170.8 7.7 %copy-start.2 = (s32[2048]{0:T(1024)S(1)}, s32[2048]{0:T(1024)}, u32[]{:S(2)}) copy-start(s32[2048]{0:T(1024)} %param.14) | copy-start | bytes 24580
  170.9 121.2 %all-to-all-start.1 = ((bf16[32,512,256]{2,1,0:T(8,128)(2,1)}), bf16[32,512,256]{2,1,0:T(8,128)(2,1)}, u32[]{:S(2)}, u32[]{:S(2)}) async-start(bf16[32,512,256]{2,1,0:T(8,128)(2,1)} %broadcast_select_fusion), calls=%async_computation.1 | async-start | bytes 16777216 | tf_op jit(solution)/shard_map/all_to_all | solution.py:76
  292.0 77.3 %all-to-all-start.2 = ((s32[32,1,128]{2,1,0:T(1,128)}), s32[32,1,128]{2,1,0:T(1,128)S(1)}, u32[]{:S(2)}, u32[]{:S(2)}) async-start(s32[32,1,128]{2,1,0:T(1,128)} %bitcast.11), calls=%async_computation.2 | async-start | bytes 32768 | tf_op jit(solution)/shard_map/all_to_all | solution.py:109
  306.3 54.2 %copy-start = (bf16[2048,256]{1,0:T(8,128)(2,1)S(1)}, bf16[2048,256]{1,0:T(8,128)(2,1)}, u32[]{:S(2)}) copy-start(bf16[2048,256]{1,0:T(8,128)(2,1)} %param.13) | copy-start | bytes 3145732
  360.9 1.0 copy-start.1
  369.3 36.3 %copy-start.4 = (bf16[256,256]{1,0:T(8,128)(2,1)S(1)}, bf16[256,256]{1,0:T(8,128)(2,1)}, u32[]{:S(2)}) copy-start(bf16[256,256]{1,0:T(8,128)(2,1)} %param.15) | copy-start | bytes 393220
  369.3 36.3 %all-to-all-start.3 = ((bf16[32,128,256]{2,1,0:T(8,128)(2,1)}), bf16[32,128,256]{2,1,0:T(8,128)(2,1)S(1)}, u32[]{:S(2)}, u32[]{:S(2)}) async-start(bf16[32,128,256]{2,1,0:T(8,128)(2,1)} %bitcast.13), calls=%async_computation.3 | async-start | bytes 4194304 | tf_op jit(solution)/shard_map/all_to_all | solution.py:102
